TPU v7x, 32 devices: a whole 2x2x4 slice. The times are simulated.
32 devices in a mesh: region: 8 (over z, y), depth: 4 (over x, core).
Axes of the slice: x: 2, y: 2, z: 4, core: 2. Of those that a mesh axis runs over, the one named last changes fastest.
Arguments:
- displacement: float32 [16, 16, 3, 1024], P('depth', None, None, 'region'), may hold values from -1.5 to 1.5
- velocity: float32 [16, 16, 3, 1024], P('depth', None, None, 'region'), may hold values from -4 to 4
- growth: float32 [16, 16, 1024], P('depth', None, 'region'), may hold values from 1 to 1.6
- shear_modulus: float32 [16, 16, 1024], P('depth', None, 'region'), may hold values from 0.3 to 3
- pair_slots: int32 [4, 8, 3, 16], P('depth', 'region'), may hold values from 0 to 63, as said below
- pair_count: int32 [4, 8], P('depth', 'region'), may hold values from 12 to 16, as said below
- separation: float32 [4, 8, 3, 16], P('depth', 'region'), may hold values from -1 to 1, as said below
Outputs:
- new_velocity: float32 [16, 16, 3, 1024], P('depth', None, None, 'region')
- new_displacement: float32 [16, 16, 3, 1024], P('depth', None, None, 'region')
Inputs may be any that keep to these rules, and one draw needn't show every extreme that they name: `pair_slots`: row 0 of a slot is a patch of the own region below 64, row 1 a region, row 2 a patch of that region below 64. Slots k < pair_count[s, r] are live and name another region; the rest hold arbitrary values in the same ranges. Contact is symmetric: a live slot (l, m, q) with separation o on (s, r) comes with a live slot (q, r, l) with separation -o on (s, m). At most 4 live slots of one region and slab name the same region; in every slab some region has exactly 4 live slots for every region it names. `pair_count`: in every slab some region has 16 live slots. `separation`: opposite on the two sides of a contact, as stated for pair_slots.
All inputs are finite; a program needn't handle non-finite values.
Results may differ from a plain program's by a relative error of at most 0.0003.
Values sent between devices are 32-bit elements; how exact they have to be, the bound alone decides.
No kernel may reach another device: no remote copies, remote signals or barrier semaphores. Data moves between devices by JAX's collectives and lax.ppermute only.
A program may use at most 64 MiB of HBM per device.

v0:
```python
import math
import jax
import jax.numpy as jnp
from jax import lax
from jax.sharding import PartitionSpec as P

CAP = 4
PERMUTATIONS = ((0, 1, 2), (0, 2, 1), (1, 0, 2), (1, 2, 0), (2, 0, 1), (2, 1, 0))
CORNER_SET = (
    (0, 0, 0),
    (0, 0, 1),
    (0, 1, 0),
    (0, 1, 1),
    (1, 0, 0),
    (1, 0, 1),
    (1, 1, 0),
    (1, 1, 1),
)
REST_VOLUME = 1.0 / 6.0
STEP_TIME = 0.2


def with_halo(cells, sides, width):
    for axis, dim in sides:
        count = lax.axis_size(axis)
        head = lax.slice_in_dim(cells, 0, width, axis=dim)
        tail = lax.slice_in_dim(cells, cells.shape[dim] - width, cells.shape[dim], axis=dim)
        cells = jnp.concatenate(
            [
                lax.ppermute(tail, axis, [(i, (i + 1) % count) for i in range(count)]),
                cells,
                lax.ppermute(head, axis, [((i + 1) % count, i) for i in range(count)]),
            ],
            axis=dim,
        )
    return cells


def unit_step(component):
    return tuple((1 if position == 2 - component else 0 for position in range(3)))


def joined(first_offset, second_offset):
    return tuple((first_offset[index] + second_offset[index] for index in range(3)))


def shifted(field, offset):
    return jnp.roll(field, (-offset[0], -offset[1], -offset[2]), axis=(0, 1, 2))


def cell_forces(displacement, growth, shear, valid):
    fields = [displacement[:, :, index, :] for index in range(3)]
    corners = {offset: [shifted(field, offset) for field in fields] for offset in CORNER_SET}
    inverse = 1.0 / growth
    squared = growth * growth
    weight = valid * REST_VOLUME
    totals = {offset: [jnp.zeros_like(growth) for index in range(3)] for offset in CORNER_SET}
    for ordering in PERMUTATIONS:
        first_axis, second_axis, third_axis = ordering
        start = (0, 0, 0)
        middle = unit_step(first_axis)
        upper = joined(middle, unit_step(second_axis))
        summit = (1, 1, 1)
        columns = [None, None, None]
        columns[first_axis] = [corners[middle][row] - corners[start][row] for row in range(3)]
        columns[second_axis] = [corners[upper][row] - corners[middle][row] for row in range(3)]
        columns[third_axis] = [corners[summit][row] - corners[upper][row] for row in range(3)]
        elastic_f = [
            [
                (columns[col][row] + (1.0 if row == col else 0.0)) * (inverse if col < 2 else 1.0)
                for col in range(3)
            ]
            for row in range(3)
        ]
        cofactor = [
            [
                elastic_f[(row + 1) % 3][(col + 1) % 3] * elastic_f[(row + 2) % 3][(col + 2) % 3]
                - elastic_f[(row + 1) % 3][(col + 2) % 3] * elastic_f[(row + 2) % 3][(col + 1) % 3]
                for col in range(3)
            ]
            for row in range(3)
        ]
        jacobian = (
            elastic_f[0][0] * cofactor[0][0]
            + elastic_f[0][1] * cofactor[0][1]
            + elastic_f[0][2] * cofactor[0][2]
        )
        pressure = 4.0 * (jacobian - 1.25)
        stress = [
            [
                shear
                * (elastic_f[row][col] + pressure * cofactor[row][col])
                * (growth if col < 2 else squared)
                * weight
                for col in range(3)
            ]
            for row in range(3)
        ]
        for row in range(3):
            col_first = stress[row][first_axis]
            col_second = stress[row][second_axis]
            col_third = stress[row][third_axis]
            totals[start][row] = totals[start][row] + col_first
            totals[middle][row] = totals[middle][row] + (col_second - col_first)
            totals[upper][row] = totals[upper][row] + (col_third - col_second)
            totals[summit][row] = totals[summit][row] - col_third
    result = []
    for row in range(3):
        summed = jnp.zeros_like(growth)
        for offset in CORNER_SET:
            summed = summed + jnp.roll(totals[offset][row], offset, axis=(0, 1, 2))
        result.append(summed)
    return jnp.stack(result, axis=2)


def pair_forces(near, far):
    deltas = [near[:, index, :, None] - far[:, index, None, :] for index in range(3)]
    distance = deltas[0] * deltas[0] + deltas[1] * deltas[1] + deltas[2] * deltas[2]
    kernel = jnp.exp(-distance)
    return jnp.stack([jnp.sum(delta * kernel, axis=2) for delta in deltas], axis=1)


def blocked_forces(near, far):
    total_rows = near.shape[0]
    block = math.gcd(total_rows, 32)
    shaped = (total_rows // block, block) + near.shape[1:]
    result = lax.map(
        lambda couple: pair_forces(couple[0], couple[1]),
        (near.reshape(shaped), far.reshape(shaped)),
    )
    return result.reshape(near.shape)


def local(displacement, velocity, growth, shear_modulus, pair_slots, pair_count, separation):
    slab_len, width_y, _, patch_len = displacement.shape
    regions = lax.axis_size("region")
    slabs = lax.axis_size("depth")
    depth_index = lax.axis_index("depth")
    stacked = jnp.concatenate(
        [displacement, growth[:, :, None, :], shear_modulus[:, :, None, :]], axis=2
    )
    extended = with_halo(stacked, (("region", 3), ("depth", 0)), 1)
    z_local = jnp.arange(slab_len + 2, dtype=jnp.int32)
    z_global = depth_index * slab_len + z_local - 1
    z_valid = (z_local <= slab_len) & (z_global >= 0) & (z_global <= slab_len * slabs - 2)
    y_valid = jnp.arange(width_y, dtype=jnp.int32) <= width_y - 2
    x_valid = jnp.arange(patch_len + 2, dtype=jnp.int32) <= patch_len
    valid = (z_valid[:, None, None] & y_valid[None, :, None] & x_valid[None, None, :]).astype(
        jnp.float32
    )
    elastic_ext = cell_forces(
        extended[:, :, 0:3, :], extended[:, :, 3, :], extended[:, :, 4, :], valid
    )
    elastic = elastic_ext[1 : slab_len + 1, :, :, 1 : patch_len + 1]
    patches_dev = slab_len * width_y
    component_row = lax.broadcasted_iota(jnp.int32, (3, patch_len), 0)
    along_row = lax.broadcasted_iota(jnp.int32, (3, patch_len), 1).astype(jnp.float32)
    rest_line = jnp.where(component_row == 0, along_row, jnp.zeros_like(along_row))
    own_points = displacement.reshape(patches_dev, 3, patch_len) + rest_line
    slots = pair_slots[0, 0]
    own_patch = slots[0]
    peer_region = slots[1]
    peer_patch = slots[2]
    slot_total = slots.shape[1]
    offsets = jnp.transpose(separation[0, 0])
    live = jnp.arange(slot_total, dtype=jnp.int32) < pair_count[0, 0]
    onehot_peer = (
        (peer_region[:, None] == jnp.arange(regions, dtype=jnp.int32)[None, :]) & live[:, None]
    ).astype(jnp.int32)
    before = jnp.cumsum(onehot_peer, axis=0) - onehot_peer
    rank = jnp.sum(before * onehot_peer, axis=1)
    buckets = regions * CAP
    bucket = jnp.where(live, peer_region * CAP + rank, buckets)
    outgoing = (
        jnp.zeros((buckets, 3, patch_len), jnp.float32)
        .at[bucket]
        .set(own_points[own_patch] - offsets[:, :, None], mode="drop")
    )
    labels = (
        jnp.full((buckets,), -1.0, jnp.float32)
        .at[bucket]
        .set(peer_patch.astype(jnp.float32), mode="drop")
    )
    arrived, arrived_labels = (
        lax.all_to_all(
            outgoing.reshape(regions, CAP, 3, patch_len),
            "region",
            split_axis=0,
            concat_axis=0,
            tiled=True,
        ),
        lax.all_to_all(
            labels.reshape(regions, CAP), "region", split_axis=0, concat_axis=0, tiled=True
        ),
    )
    arrived = arrived.reshape(buckets, 3, patch_len)
    arrived_labels = arrived_labels.reshape(buckets)
    chosen = arrived_labels >= 0.0
    targets = jnp.where(chosen, arrived_labels, 0.0).astype(jnp.int32)
    forces = blocked_forces(own_points[targets], arrived) * chosen[:, None, None].astype(
        jnp.float32
    )
    selector = (
        (targets[:, None] == jnp.arange(patches_dev, dtype=jnp.int32)[None, :]) & chosen[:, None]
    ).astype(jnp.float32)
    contact = jnp.einsum("kp,kcx->pcx", selector, forces, precision=lax.Precision.HIGHEST)
    contact = contact.reshape(slab_len, width_y, 3, patch_len)
    new_velocity = velocity + STEP_TIME * (elastic + contact)
    new_displacement = displacement + STEP_TIME * new_velocity
    return (new_velocity, new_displacement)


def solution(mesh):
    in_specs = (
        P("depth", None, None, "region"),
        P("depth", None, None, "region"),
        P("depth", None, "region"),
        P("depth", None, "region"),
        P("depth", "region", None, None),
        P("depth", "region"),
        P("depth", "region", None, None),
    )
    out_specs = (P("depth", None, None, "region"), P("depth", None, None, "region"))
    return jax.shard_map(local, mesh=mesh, in_specs=in_specs, out_specs=out_specs, check_vma=False)
```

profile of v0, /device:TPU:1, one launch (start us, length us, event | category | flops | bytes accessed | tf_op | source)
XLA Modules:
  0.0 50.1 jit_solution(1736963173095069045)
XLA Ops:
  1.3 0.7 %convert_bitcast_fusion = (f32[16]{0:T(128)S(1)}, s32[16]{0:T(128)S(1)}) fusion(s32[1,1,3,16]{3,1,2,0:T(1,128)} %param.11), kind=kLoop, calls=%fused_computation.623 | loop fusion | flops 16 | bytes 256 | tf_op jit(solution)/shard_map/convert_element_type | solution.py:182
  2.3 0.7 %fusion.163 = (s32[16]{0:T(128)S(1)}, s32[16]{0:T(128)S(1)}) fusion(s32[1,1,3,16]{3,1,2,0:T(1,128)} %param.11, s32[16]{0:T(128)S(1)} %select_reduce_fusion, s32[]{:T(128)} %bitcast.952), kind=kLoop, calls=%fused_computation.618 | loop fusion | flops 160 | bytes 324 | tf_op jit(solution)/shard_map/select_n | solution.py:177
  2.9 0.6 %scatter_custom_fusion = f32[32]{0:T(128)S(1)} fusion(s32[16]{0:T(128)S(1)} %get-tuple-element.149, f32[16]{0:T(128)S(1)} %get-tuple-element.146, f32[]{:T(128)} %constant.30.clone.1), kind=kCustom, calls=%fused_computation.629 | custom fusion | bytes 132 | tf_op jit(solution)/shard_map/scatter | solution.py:182
  3.6 0.7 %all_to_all.9 = f32[8,1,4]{2,0,1:T(8,128)} reshape(f32[32]{0:T(128)S(1)} %scatter_custom_fusion) | data formatting | bytes 256 | tf_op jit(solution)/shard_map/all_to_all | solution.py:192
  4.3 6.4 %all-to-all-start = ((f32[8,1,4]{2,1,0:T(1,128)}), f32[8,1,4]{2,1,0:T(1,128)S(1)}, u32[]{:S(2)}, u32[]{:S(2)}) async-start(f32[8,1,4]{2,1,0:T(1,128)} %bitcast.104), calls=%async_computation | async-start | bytes 8192 | tf_op jit(solution)/shard_map/all_to_all | solution.py:192
  10.6 1.0 %pad_maximum_fusion.10 = f32[4,16,5,128]{3,1,0,2:T(8,128)S(1)} fusion(f32[4,16,1,128]{3,1,0,2:T(8,128)} %bitcast.1004, f32[4,16,1,128]{3,1,0,2:T(8,128)} %bitcast.1008, f32[4,16,3,128]{3,1,2,0:T(8,128)} %param.7), kind=kLoop, calls=%fused_computation.108 | loop fusion | flops 81920 | bytes 327680 | tf_op jit(solution)/shard_map/concatenate | solution.py:139
  11.7 1.5 %collective-permute-start = (f32[4,16,5,1]{3,1,0,2:T(8,128)S(1)}, f32[4,16,5,1]{3,1,0,2:T(8,128)S(1)}, u32[]{:S(2)}, u32[]{:S(2)}) collective-permute-start(f32[4,16,5,1]{3,1,0,2:T(8,128)S(1)} %get-tuple-element.108), channel_id=1, source_target_pairs={{0,4},{4,8},{8,12},{12,16},{16,20},{20,24},{24,28},{28,0},{1,5},{5... | collective-permute-start | bytes 3848 | tf_op jit(solution)/shard_map/ppermute | solution.py:30
  13.2 2.8 %collective-permute-start.1 = (f32[4,16,5,1]{3,1,0,2:T(8,128)S(1)}, f32[4,16,5,1]{3,1,0,2:T(8,128)S(1)}, u32[]{:S(2)}, u32[]{:S(2)}) collective-permute-start(f32[4,16,5,1]{3,1,0,2:T(8,128)S(1)} %get-tuple-element.109), channel_id=1, source_target_pairs={{4,0},{8,4},{12,8},{16,12},{20,16},{24,20},{28,24},{0,28},{5,1},{9... | collective-permute-start | bytes 3848 | tf_op jit(solution)/shard_map/ppermute | solution.py:32
  16.4 0.6 %gather_fusion.1 = f32[16,3,128]{2,1,0:T(4,128)S(1)} fusion(f32[64,3,128]{2,1,0:T(4,128)S(1)} %copy_add_fusion, s32[1024]{0:T(1024)S(1)} %pad_clamp_fusion), kind=kCustom, calls=%fused_computation.1 | custom fusion | bytes 49216 | tf_op jit(solution)/shard_map/gather | solution.py:177
  17.1 1.0 %scatter_fusion = f32[32,3,128]{2,1,0:T(4,128)S(1)} fusion(f32[32,3,128]{2,1,0:T(4,128)S(1)} %broadcast_in_dim.24, s32[16]{0:T(128)S(1)} %get-tuple-element.149, f32[16,3,128]{2,1,0:T(4,128)S(1)} %broadcast_subtract_fusion), kind=kCustom, calls=%fused_computation.3 | custom fusion | bytes 73792 | tf_op jit(solution)/shard_map/scatter | solution.py:177
  18.2 0.6 %copy.222 = f32[8,4,3,128]{3,1,2,0:T(4,128)} copy(f32[8,4,3,128]{3,2,1,0:T(4,128)S(1)} %bitcast.1018) | data formatting | bytes 98304 | tf_op jit(solution)/shard_map/reshape | solution.py:186
  18.8 3.3 %all-to-all-start.1 = ((f32[8,4,3,128]{3,1,2,0:T(4,128)}), f32[8,4,3,128]{3,1,2,0:T(4,128)S(1)}, u32[]{:S(2)}, u32[]{:S(2)}) async-start(f32[8,4,3,128]{3,1,2,0:T(4,128)} %copy.222), calls=%async_computation.1 | async-start | bytes 98304 | tf_op jit(solution)/shard_map/all_to_all | solution.py:185
  22.3 0.5 %broadcast.1172 = f32[]{:T(128)} broadcast(f32[]{:T(128)} %constant.1063), dimensions={} | broadcast | bytes 8 | tf_op jit(solution)/shard_map/all_to_all | solution.py:192
  22.8 0.7 %reduce.5 = f32[8,4]{1,0:T(8,128)S(1)} reduce(f32[8,1,4]{2,1,0:T(1,128)S(1)} %all-to-all-done, f32[]{:T(128)} %broadcast.1172), dimensions={1}, to_apply=%all_to_all.10.reduce_sub_computation.5 | reduce | bytes 260 | tf_op jit(solution)/shard_map/all_to_all | solution.py:192
  23.5 0.6 %gather_fusion = f32[32,3,128]{2,1,0:T(4,128)S(1)} fusion(f32[64,3,128]{2,1,0:T(4,128)S(1)} %copy_add_fusion, s32[1024]{0:T(1024)S(1)} %pad_clamp_fusion.1), kind=kCustom, calls=%fused_computation | custom fusion | bytes 98432 | tf_op jit(solution)/shard_map/gather | solution.py:200
  24.4 2.7 %collective-permute-start.2 = (f32[1,16,5,130]{3,1,0,2:T(8,128)S(1)}, f32[1,16,5,130]{3,1,0,2:T(8,128)S(1)}, u32[]{:S(2)}, u32[]{:S(2)}) collective-permute-start(f32[1,16,5,130]{3,1,0,2:T(8,128)S(1)} %get-tuple-element.106), channel_id=1, source_target_pairs={{0,1},{1,2},{2,3},{3,0},{4,5},{5,6},{6,7},{7,4},{8,9},{9,10},{10,1... | collective-permute-start | bytes 124808 | tf_op jit(solution)/shard_map/ppermute | solution.py:30
  27.0 1.5 %collective-permute-done.2 = f32[1,16,5,130]{3,1,0,2:T(8,128)S(1)} collective-permute-done((f32[1,16,5,130]{3,1,0,2:T(8,128)S(1)}, f32[1,16,5,130]{3,1,0,2:T(8,128)S(1)}, u32[]{:S(2)}, u32[]{:S(2)}) %collective-permute-start.2) | collective-permute-done | bytes 41632 | tf_op jit(solution)/shard_map/ppermute | solution.py:30
  28.5 2.4 %collective-permute-done.3 = f32[1,16,5,130]{3,1,0,2:T(8,128)S(1)} collective-permute-done((f32[1,16,5,130]{3,1,0,2:T(8,128)S(1)}, f32[1,16,5,130]{3,1,0,2:T(8,128)S(1)}, u32[]{:S(2)}, u32[]{:S(2)}) %collective-permute-start.3) | collective-permute-done | bytes 41632 | tf_op jit(solution)/shard_map/ppermute | solution.py:32
  33.3 1.2 %subtract_subtract_fusion.2 = (f32[6,16,130]{2,1,0:T(8,128)S(1)}, f32[6,16,130]{2,1,0:T(8,128)S(1)}, f32[6,16,130]{2,1,0:T(8,128)S(1)}, f32[6,16,130]{2,1,0:T(8,...) fusion(pred[130]{0:T(512)(128)(4,1)S(1)} %iota_compare_fusion.1, ...), kind=kLoop, calls=%fused_computation.403 | loop fusion | flops 2857920 | bytes 4043746 | tf_op jit(solution)/shard_map/sub | solution.py:106
  34.7 0.3 fusion.70
  35.3 0.3 fusion.61
  35.6 0.3 subtract_add_fusion
  36.5 0.3 subtract_add_fusion.2
  36.7 0.3 subtract_add_fusion.5
  37.0 0.6 %subtract_subtract_fusion.1 = f32[6,16,130]{2,1,0:T(8,128)S(1)} fusion(f32[6,16,130]{2,1,0:T(8,128)S(1)} %get-tuple-element.97, f32[6,16,130]{2,1,0:T(8,128)S(1)} %get-tuple-element.99, f32[6,16,130]{2,1,0:T(8,128)S(1)} %get-tuple-element.98, f32[6,16,130]{2,1,0:T(8,128)S(1)} %get-tuple-element.87, f32[6,16,130]{2,1,0:T(8,128)S(1)} %get-tuple-element.85, ...), kind=kLoop, calls=%fused_computation.399 | loop fusion | flops 1235520 | bytes 2246626 | tf_op jit(solution)/shard_map/sub | solution.py:106
  37.6 0.6 %subtract_subtract_fusion = f32[6,16,130]{2,1,0:T(8,128)S(1)} fusion(f32[6,16,130]{2,1,0:T(8,128)S(1)} %get-tuple-element.89, f32[6,16,130]{2,1,0:T(8,128)S(1)} %get-tuple-element.85, f32[6,16,130]{2,1,0:T(8,128)S(1)} %get-tuple-element.95, f32[6,16,130]{2,1,0:T(8,128)S(1)} %get-tuple-element.98, f32[6,16,130]{2,1,0:T(8,128)S(1)} %get-tuple-element.90, ...), kind=kLoop, calls=%fused_computation.391 | loop fusion | flops 1235520 | bytes 2246626 | tf_op jit(solution)/shard_map/sub | solution.py:106
  39.7 0.6 %slice-done = f32[1,16,130]{2,1,0:T(8,128)S(1)} async-done(((f32[6,16,130]{2,1,0:T(8,128)}), f32[1,16,130]{2,1,0:T(8,128)S(1)}, s32[]{:S(2)}) %slice-start) | async-done | bytes 8344 | tf_op jit(solution)/shard_map/jit(_roll_static)/slice | solution.py:111
  42.6 1.0 %fusion.22 = (f32[6,16,1,130]{3,1,2,0:T(8,128)S(1)}, f32[6,16,1,130]{3,1,0,2:T(8,128)S(1)}, f32[6,16,1,130]{3,1,0,2:T(8,128)S(1)}, f32[6,16,1,130]{3,1,0,2:T(8,1...) fusion(f32[6,16,1,129]{3,1,0,2:T(8,128)S(1)} %slice_bitcast_fus, ...), kind=kLoop, calls=%fused_computation.138 | loop fusion | flops 2882880 | bytes 3045346 | tf_op jit(solution)/shard_map/add | solution.py:111
  43.6 0.8 %fusion.30 = f32[6,16,1,130]{3,1,2,0:T(8,128)S(1)} fusion(f32[6,16,1,129]{3,1,0,2:T(8,128)S(1)} %slice_bitcast_fusion.2, f32[6,16,1,1]{3,1,0,2:T(8,128)S(1)} %slice_bitcast_fusion.16, f32[6,15,1,130]{3,1,0,2:T(8,128)S(1)} %slice_bitcast_fusion.1, f32[6,1,1,130]{3,1,0,2:T(1,128)S(1)} %slice_bitcast_fusion.27, f32[6,16,1,129]{3,1,0,2:T(8,128)S(1)} %fusion.75, ...), kind=kLoop, calls=%fused_computation.146 | loop fusion | flops 2283840 | bytes 2446306 | tf_op jit(solution)/shard_map/add | solution.py:111
  44.5 0.8 %fusion.38 = f32[6,16,1,130]{3,1,2,0:T(8,128)S(1)} fusion(f32[6,16,1,129]{3,1,0,2:T(8,128)S(1)} %slice_bitcast_fusion.5, f32[6,16,1,1]{3,1,0,2:T(8,128)S(1)} %slice_bitcast_fusion.18, f32[6,15,1,130]{3,1,0,2:T(8,128)S(1)} %slice_bitcast_fusion.4, f32[6,1,1,130]{3,1,0,2:T(1,128)S(1)} %slice_bitcast_fusion.28, f32[6,16,1,129]{3,1,0,2:T(8,128)S(1)} %fusion.79, ...), kind=kLoop, calls=%fused_computation.154 | loop fusion | flops 2283840 | bytes 2446306 | tf_op jit(solution)/shard_map/add | solution.py:111
  45.4 3.8 %fusion.4 = (f32[32,128]{1,0:T(8,128)S(1)}, f32[32,128]{1,0:T(8,128)S(1)}, f32[32,128]{1,0:T(8,128)S(1)}) fusion(f32[32,128]{1,0:T(8,128)S(1)} %get-tuple-element.144, f32[32,128]{1,0:T(8,128)S(1)} %bitcast.1036, f32[32,128]{1,0:T(8,128)S(1)} %get-tuple-element.145, f32[32,128]{1,0:T(8,128)S(1)} %bitcast.1035, f32[32,128]{1,0:T(8,128)S(1)} %get-tuple-element.143, ...), kind=kLoop, calls=%fused_computation.14 | loop fusion | flops 7852032 | bytes 147456 | tf_op jit(solution)/shard_map/while/body/eval_jaxpr/reduce_sum | solution.py:120
  49.2 0.9 %multiply_add_fusion = (f32[4,16,3,128]{3,1,2,0:T(8,128)}, f32[4,16,3,128]{3,1,2,0:T(8,128)}) fusion(f32[4,16,3,128]{3,1,2,0:T(8,128)S(1)} %copy-done, f32[4,16,3,128]{3,1,2,0:T(8,128)S(1)} %copy-done.4, f32[32,1,128]{2,0,1:T(8,128)S(1)} %bitcast.1032, f32[32,1,128]{2,0,1:T(8,128)S(1)} %bitcast.1033, f32[32,1,128]{2,0,1:T(8,128)S(1)} %bitcast.1031, ...), kind=kOutput, calls=%fused_computation.390 | convolution fusion | flops 9650176 | bytes 592672 | tf_op jit(solution)/shard_map/kp,kcx->pcx/dot_general | solution.py:206
  (161 shorter events, 7.8 us)
Async XLA Ops:
  4.3 14.6 %all-to-all-start = ((f32[8,1,4]{2,1,0:T(1,128)}), f32[8,1,4]{2,1,0:T(1,128)S(1)}, u32[]{:S(2)}, u32[]{:S(2)}) async-start(f32[8,1,4]{2,1,0:T(1,128)} %bitcast.104), calls=%async_computation | async-start | bytes 8192 | tf_op jit(solution)/shard_map/all_to_all | solution.py:192
  10.6 5.4 %copy-start = (f32[4,16,3,128]{3,1,2,0:T(8,128)S(1)}, f32[4,16,3,128]{3,1,2,0:T(8,128)}, u32[]{:S(2)}) copy-start(f32[4,16,3,128]{3,1,2,0:T(8,128)} %param.7) | copy-start | bytes 294916
  11.6 4.5 %copy-start.5 = (f32[1,1,3,16]{3,1,2,0:T(1,128)S(1)}, f32[1,1,3,16]{3,1,2,0:T(1,128)}, u32[]{:S(2)}) copy-start(f32[1,1,3,16]{3,1,2,0:T(1,128)} %param.13) | copy-start | bytes 580
  11.7 12.5 %collective-permute-start = (f32[4,16,5,1]{3,1,0,2:T(8,128)S(1)}, f32[4,16,5,1]{3,1,0,2:T(8,128)S(1)}, u32[]{:S(2)}, u32[]{:S(2)}) collective-permute-start(f32[4,16,5,1]{3,1,0,2:T(8,128)S(1)} %get-tuple-element.108), channel_id=1, source_target_pairs={{0,4},{4,8},{8,12},{12,16},{16,20},{20,24},{24,28},{28,0},{1,5},{5... | collective-permute-start | bytes 3848 | tf_op jit(solution)/shard_map/ppermute | solution.py:30
  13.2 11.0 %collective-permute-start.1 = (f32[4,16,5,1]{3,1,0,2:T(8,128)S(1)}, f32[4,16,5,1]{3,1,0,2:T(8,128)S(1)}, u32[]{:S(2)}, u32[]{:S(2)}) collective-permute-start(f32[4,16,5,1]{3,1,0,2:T(8,128)S(1)} %get-tuple-element.109), channel_id=1, source_target_pairs={{4,0},{8,4},{12,8},{16,12},{20,16},{24,20},{28,24},{0,28},{5,1},{9... | collective-permute-start | bytes 3848 | tf_op jit(solution)/shard_map/ppermute | solution.py:32
  16.4 7.9 %copy-start.1 = (f32[4,16,128]{2,1,0:T(8,128)S(1)}, f32[4,16,128]{2,1,0:T(8,128)}, u32[]{:S(2)}) copy-start(f32[4,16,128]{2,1,0:T(8,128)} %param.10) | copy-start | bytes 98308
  16.4 7.9 %copy-start.2 = (f32[4,16,128]{2,1,0:T(8,128)S(1)}, f32[4,16,128]{2,1,0:T(8,128)}, u32[]{:S(2)}) copy-start(f32[4,16,128]{2,1,0:T(8,128)} %param.9) | copy-start | bytes 98308
  18.8 26.5 %all-to-all-start.1 = ((f32[8,4,3,128]{3,1,2,0:T(4,128)}), f32[8,4,3,128]{3,1,2,0:T(4,128)S(1)}, u32[]{:S(2)}, u32[]{:S(2)}) async-start(f32[8,4,3,128]{3,1,2,0:T(4,128)} %copy.222), calls=%async_computation.1 | async-start | bytes 98304 | tf_op jit(solution)/shard_map/all_to_all | solution.py:185
  24.4 4.2 %collective-permute-start.2 = (f32[1,16,5,130]{3,1,0,2:T(8,128)S(1)}, f32[1,16,5,130]{3,1,0,2:T(8,128)S(1)}, u32[]{:S(2)}, u32[]{:S(2)}) collective-permute-start(f32[1,16,5,130]{3,1,0,2:T(8,128)S(1)} %get-tuple-element.106), channel_id=1, source_target_pairs={{0,1},{1,2},{2,3},{3,0},{4,5},{5,6},{6,7},{7,4},{8,9},{9,10},{10,1... | collective-permute-start | bytes 124808 | tf_op jit(solution)/shard_map/ppermute | solution.py:30
  27.0 3.9 %collective-permute-start.3 = (f32[1,16,5,130]{3,1,0,2:T(8,128)S(1)}, f32[1,16,5,130]{3,1,0,2:T(8,128)S(1)}, u32[]{:S(2)}, u32[]{:S(2)}) collective-permute-start(f32[1,16,5,130]{3,1,0,2:T(8,128)S(1)} %get-tuple-element.107), channel_id=1, source_target_pairs={{1,0},{2,1},{3,2},{0,3},{5,4},{6,5},{7,6},{4,7},{9,8},{10,9},{11,1... | collective-permute-start | bytes 124808 | tf_op jit(solution)/shard_map/ppermute | solution.py:32
  38.2 1.3 %copy-start.3 = (f32[6,16,130]{2,1,0:T(8,128)}, f32[6,16,130]{2,1,0:T(8,128)S(1)}, u32[]{:S(2)}) copy-start(f32[6,16,130]{2,1,0:T(8,128)S(1)} %subtract_subtract_fusion) | copy-start | bytes 149764
  39.5 0.7 %slice-start = ((f32[6,16,130]{2,1,0:T(8,128)}), f32[1,16,130]{2,1,0:T(8,128)S(1)}, s32[]{:S(2)}) async-start(f32[6,16,130]{2,1,0:T(8,128)} %copy-done.3), calls=%async_computation.2 | async-start | bytes 32768 | tf_op jit(solution)/shard_map/jit(_roll_static)/slice | solution.py:111
  39.5 0.9 %slice-start.1 = ((f32[6,16,130]{2,1,0:T(8,128)}), f32[5,16,130]{2,1,0:T(8,128)S(1)}, s32[]{:S(2)}) async-start(f32[6,16,130]{2,1,0:T(8,128)} %copy-done.3), calls=%async_computation.3 | async-start | bytes 163840 | tf_op jit(solution)/shard_map/jit(_roll_static)/slice | solution.py:111
  45.4 3.8 %copy-start.4 = (f32[4,16,3,128]{3,1,2,0:T(8,128)S(1)}, f32[4,16,3,128]{3,1,2,0:T(8,128)}, u32[]{:S(2)}) copy-start(f32[4,16,3,128]{3,1,2,0:T(8,128)} %param.8) | copy-start | bytes 294916
where the time goes:
time: 50.5 us; the launch traced here: 50.1 us
  other arithmetic  19.6 us (39%)
  starting transfers between devices  16.7 us (33%)
  local copies, waits for them, and re-layouts  6.76 us (13%)
  waiting for transfers between devices  3.87 us (8%)
  between operations  2.34 us (5%)
  matrix products  0.94 us (2%)
    all_to_all x1, starting transfers between devices, local(): lax.all_to_all(labels.reshape(regions, CAP), 'region', split_axis=0, conc...  6.37 us
    ppermute x2, starting transfers between devices, with_halo(): lax.ppermute(tail, axis, [(i, (i + 1) % count) for i in range(count)])  4.18 us
    reduce_sum x1, other arithmetic, pair_forces(): jnp.sum(delta * kernel, axis=2)  3.82 us
    all_to_all x1, starting transfers between devices, local(): lax.all_to_all(outgoing.reshape(regions, CAP, 3, patch_len), 'region', sp...  3.35 us
    ppermute x2, starting transfers between devices, with_halo(): lax.ppermute(head, axis, [((i + 1) % count, i) for i in range(count)])  2.77 us
    add x3, other arithmetic, cell_forces(): summed = summed + jnp.roll(totals[offset][row], offset, axis=(0, 1, 2))  2.72 us
    sub x3, other arithmetic, cell_forces(): totals[summit][row] = totals[summit][row] - col_third  2.38 us
    ppermute x2, waiting for transfers between devices, with_halo(): lax.ppermute(head, axis, [((i + 1) % count, i) for i in range(count)])  2.38 us
  transfers between devices with their start and end apart: 6, of which 2 were waited for; matrix products, arithmetic and copies ran while one was open for 37% of the time, Pallas kernels for 0%

commit v1 on v0

--- a/solution.py
+++ b/solution.py
@@ -18,6 +18,18 @@
 )
 REST_VOLUME = 1.0 / 6.0
 STEP_TIME = 0.2
+
+
+def exchange_directly(x, axis, split, join):
+    ways, here = (lax.axis_size(axis), lax.axis_index(axis))
+    width = x.shape[split] // ways
+    turned = jnp.roll(x, -here * width, axis=split)
+    got = [lax.slice_in_dim(turned, 0, width, axis=split)]
+    for far in range(1, ways):
+        sent = lax.slice_in_dim(turned, far * width, (far + 1) * width, axis=split)
+        got.append(lax.ppermute(sent, axis, [(d, (d + far) % ways) for d in range(ways)]))
+    line = jnp.concatenate(got[::-1], axis=join)
+    return jnp.roll(line, (here + 1) * got[0].shape[join], axis=join)
 
 
 def with_halo(cells, sides, width):
@@ -182,13 +194,7 @@
         .set(peer_patch.astype(jnp.float32), mode="drop")
     )
     arrived, arrived_labels = (
-        lax.all_to_all(
-            outgoing.reshape(regions, CAP, 3, patch_len),
-            "region",
-            split_axis=0,
-            concat_axis=0,
-            tiled=True,
-        ),
+        exchange_directly(outgoing.reshape(regions, CAP, 3, patch_len), "region", 0, 0),
         lax.all_to_all(
             labels.reshape(regions, CAP), "region", split_axis=0, concat_axis=0, tiled=True
         ),

time: 50.5 us -> 63 us (1.25)
  the two profiles are of different devices: /device:TPU:1 before, /device:TPU:29 now
where the time goes in v1:
time: 63 us; the launch traced here: 62.7 us
  starting transfers between devices  21 us (33%)
  other arithmetic  19.8 us (31%)
  waiting for transfers between devices  12.2 us (19%)
  local copies, waits for them, and re-layouts  6.25 us (10%)
  between operations  2.42 us (4%)
  matrix products  0.93 us (1%)
    ppermute x7, waiting for transfers between devices, exchange_directly(): lax.ppermute(sent, axis, [(d, (d + far) % ways) for d in range(ways)])  12.2 us
    ppermute x2, starting transfers between devices, with_halo(): lax.ppermute(tail, axis, [(i, (i + 1) % count) for i in range(count)])  7.47 us
    ppermute x7, starting transfers between devices, exchange_directly(): lax.ppermute(sent, axis, [(d, (d + far) % ways) for d in range(ways)])  6.66 us
    all_to_all x1, starting transfers between devices, local(): lax.all_to_all(labels.reshape(regions, CAP), 'region', split_axis=0, conc...  5.44 us
    reduce_sum x1, other arithmetic, pair_forces(): jnp.sum(delta * kernel, axis=2)  4 us
    add x3, other arithmetic, cell_forces(): summed = summed + jnp.roll(totals[offset][row], offset, axis=(0, 1, 2))  2.72 us
    sub x3, other arithmetic, cell_forces(): totals[summit][row] = totals[summit][row] - col_third  2.38 us
    add x9, other arithmetic, cell_forces(): totals[upper][row] = totals[upper][row] + (col_third - col_second)  2.09 us
  transfers between devices with their start and end apart: 12, of which 3 were waited for; matrix products, arithmetic and copies ran while one was open for 15% of the time, Pallas kernels for 0%

profile of v1, /device:TPU:29, one launch (start us, length us, event | category | flops | bytes accessed | tf_op | source)
XLA Modules:
  0.0 62.7 jit_solution(17779454078139347466)
XLA Ops:
  1.3 0.7 %convert_bitcast_fusion = (f32[16]{0:T(128)S(1)}, s32[16]{0:T(128)S(1)}) fusion(s32[1,1,3,16]{3,1,2,0:T(1,128)} %param.13), kind=kLoop, calls=%fused_computation.637 | loop fusion | flops 16 | bytes 256 | tf_op jit(solution)/shard_map/convert_element_type | solution.py:194
  2.3 0.7 %fusion.165 = (s32[16]{0:T(128)S(1)}, s32[16]{0:T(128)S(1)}) fusion(s32[1,1,3,16]{3,1,2,0:T(1,128)} %param.13, s32[16]{0:T(128)S(1)} %select_reduce_fusion, s32[]{:T(128)} %bitcast.952), kind=kLoop, calls=%fused_computation.632 | loop fusion | flops 160 | bytes 324 | tf_op jit(solution)/shard_map/select_n | solution.py:189
  2.9 0.6 scatter_custom_fusion
  3.6 0.7 %all_to_all.6 = f32[8,1,4]{2,0,1:T(8,128)} reshape(f32[32]{0:T(128)S(1)} %scatter_custom_fusion) | data formatting | bytes 256 | tf_op jit(solution)/shard_map/all_to_all | solution.py:198
  4.3 5.4 %all-to-all-start = ((f32[8,1,4]{2,1,0:T(1,128)}), f32[8,1,4]{2,1,0:T(1,128)S(1)}, u32[]{:S(2)}, u32[]{:S(2)}) async-start(f32[8,1,4]{2,1,0:T(1,128)} %bitcast.104), calls=%async_computation | async-start | bytes 8192 | tf_op jit(solution)/shard_map/all_to_all | solution.py:198
  9.7 1.0 %pad_maximum_fusion.10 = f32[4,16,5,128]{3,1,0,2:T(8,128)S(1)} fusion(f32[4,16,1,128]{3,1,0,2:T(8,128)} %bitcast.1004, f32[4,16,1,128]{3,1,0,2:T(8,128)} %bitcast.1008, f32[4,16,3,128]{3,1,2,0:T(8,128)} %param.9), kind=kLoop, calls=%fused_computation.108 | loop fusion | flops 81920 | bytes 327680 | tf_op jit(solution)/shard_map/concatenate | solution.py:151
  10.9 1.5 %collective-permute-start.1 = (f32[4,16,5,1]{3,1,0,2:T(8,128)S(1)}, f32[4,16,5,1]{3,1,0,2:T(8,128)S(1)}, u32[]{:S(2)}, u32[]{:S(2)}) collective-permute-start(f32[4,16,5,1]{3,1,0,2:T(8,128)S(1)} %get-tuple-element.110), channel_id=1, source_target_pairs={{4,0},{8,4},{12,8},{16,12},{20,16},{24,20},{28,24},{0,28},{5,1},{9... | collective-permute-start | bytes 3848 | tf_op jit(solution)/shard_map/ppermute | solution.py:44
  12.9 0.5 broadcast.1173
  13.4 0.7 %reduce.5 = f32[8,4]{1,0:T(8,128)S(1)} reduce(f32[8,1,4]{2,1,0:T(1,128)S(1)} %all-to-all-done, f32[]{:T(128)} %broadcast.1173), dimensions={1}, to_apply=%all_to_all.7.reduce_sub_computation.5 | reduce | bytes 260 | tf_op jit(solution)/shard_map/all_to_all | solution.py:198
  14.1 0.6 gather_fusion.1
  14.7 0.6 gather_fusion
  15.5 1.0 %scatter_fusion = f32[32,3,128]{2,1,0:T(4,128)S(1)} fusion(f32[32,3,128]{2,1,0:T(4,128)S(1)} %broadcast_in_dim.24, s32[16]{0:T(128)S(1)} %get-tuple-element.157, f32[16,3,128]{2,1,0:T(4,128)S(1)} %broadcast_subtract_fusion), kind=kCustom, calls=%fused_computation.3 | custom fusion | bytes 73792 | tf_op jit(solution)/shard_map/scatter | solution.py:189
  16.6 2.8 %collective-permute-start.10 = (f32[1,4,3,128]{3,1,0,2:T(4,128)S(1)}, f32[1,4,3,128]{3,1,0,2:T(4,128)S(1)}, u32[]{:S(2)}, u32[]{:S(2)}) collective-permute-start(f32[1,4,3,128]{3,1,0,2:T(4,128)S(1)} %get-tuple-element.147), channel_id=1, source_target_pairs={{0,4},{4,8},{8,12},{12,16},{16,20},{20,24},{24,28},{28,0},{1,5},{5... | collective-permute-start | bytes 18440 | tf_op jit(solution)/shard_map/ppermute | solution.py:30
  19.5 2.4 %collective-permute-start.7 = (f32[1,4,3,128]{3,1,0,2:T(4,128)S(1)}, f32[1,4,3,128]{3,1,0,2:T(4,128)S(1)}, u32[]{:S(2)}, u32[]{:S(2)}) collective-permute-start(f32[1,4,3,128]{3,1,0,2:T(4,128)S(1)} %get-tuple-element.150), channel_id=1, source_target_pairs={{0,16},{4,20},{8,24},{12,28},{16,0},{20,4},{24,8},{28,12},{1,17},{... | collective-permute-start | bytes 18440 | tf_op jit(solution)/shard_map/ppermute | solution.py:30
  21.9 1.4 %collective-permute-start.4 = (f32[1,4,3,128]{3,1,0,2:T(4,128)S(1)}, f32[1,4,3,128]{3,1,0,2:T(4,128)S(1)}, u32[]{:S(2)}, u32[]{:S(2)}) collective-permute-start(f32[1,4,3,128]{3,1,0,2:T(4,128)S(1)} %get-tuple-element.153), channel_id=1, source_target_pairs={{0,28},{4,0},{8,4},{12,8},{16,12},{20,16},{24,20},{28,24},{1,29},{... | collective-permute-start | bytes 18440 | tf_op jit(solution)/shard_map/ppermute | solution.py:30
  23.4 3.6 %collective-permute-done.4 = f32[1,4,3,128]{3,1,0,2:T(4,128)S(1)} collective-permute-done((f32[1,4,3,128]{3,1,0,2:T(4,128)S(1)}, f32[1,4,3,128]{3,1,0,2:T(4,128)S(1)}, u32[]{:S(2)}, u32[]{:S(2)}) %collective-permute-start.4) | collective-permute-done | bytes 6176 | tf_op jit(solution)/shard_map/ppermute | solution.py:30
  27.1 4.3 %collective-permute-done.5 = f32[1,4,3,128]{3,1,0,2:T(4,128)S(1)} collective-permute-done((f32[1,4,3,128]{3,1,0,2:T(4,128)S(1)}, f32[1,4,3,128]{3,1,0,2:T(4,128)S(1)}, u32[]{:S(2)}, u32[]{:S(2)}) %collective-permute-start.5) | collective-permute-done | bytes 6176 | tf_op jit(solution)/shard_map/ppermute | solution.py:30
  31.4 4.3 %collective-permute-done.6 = f32[1,4,3,128]{3,1,0,2:T(4,128)S(1)} collective-permute-done((f32[1,4,3,128]{3,1,0,2:T(4,128)S(1)}, f32[1,4,3,128]{3,1,0,2:T(4,128)S(1)}, u32[]{:S(2)}, u32[]{:S(2)}) %collective-permute-start.6) | collective-permute-done | bytes 6176 | tf_op jit(solution)/shard_map/ppermute | solution.py:30
  35.6 7.4 %collective-permute-start.2 = (f32[1,16,5,130]{3,1,0,2:T(8,128)S(1)}, f32[1,16,5,130]{3,1,0,2:T(8,128)S(1)}, u32[]{:S(2)}, u32[]{:S(2)}) collective-permute-start(f32[1,16,5,130]{3,1,0,2:T(8,128)S(1)} %get-tuple-element.107), channel_id=1, source_target_pairs={{0,1},{1,2},{2,3},{3,0},{4,5},{5,6},{6,7},{7,4},{8,9},{9,10},{10,1... | collective-permute-start | bytes 124808 | tf_op jit(solution)/shard_map/ppermute | solution.py:42
  43.2 4.0 %fusion.4 = (f32[32,128]{1,0:T(8,128)S(1)}, f32[32,128]{1,0:T(8,128)S(1)}, f32[32,128]{1,0:T(8,128)S(1)}) fusion(f32[32,128]{1,0:T(8,128)S(1)} %get-tuple-element.145, f32[32,128]{1,0:T(8,128)S(1)} %bitcast.1036, f32[32,128]{1,0:T(8,128)S(1)} %get-tuple-element.146, f32[32,128]{1,0:T(8,128)S(1)} %bitcast.1035, f32[32,128]{1,0:T(8,128)S(1)} %get-tuple-element.144, ...), kind=kLoop, calls=%fused_computation.14 | loop fusion | flops 7852032 | bytes 147456 | tf_op jit(solution)/shard_map/while/body/eval_jaxpr/reduce_sum | solution.py:132
  49.7 1.2 %subtract_subtract_fusion.2 = (f32[6,16,130]{2,1,0:T(8,128)S(1)}, f32[6,16,130]{2,1,0:T(8,128)S(1)}, f32[6,16,130]{2,1,0:T(8,128)S(1)}, f32[6,16,130]{2,1,0:T(8,...) fusion(pred[130]{0:T(512)(128)(4,1)S(1)} %iota_compare_fusion.1, ...), kind=kLoop, calls=%fused_computation.407 | loop fusion | flops 2857920 | bytes 4043746 | tf_op jit(solution)/shard_map/sub | solution.py:118
  51.0 0.3 fusion.70
  51.7 0.3 fusion.61
  52.8 0.3 subtract_add_fusion.2
  53.1 0.3 subtract_add_fusion.5
  53.4 0.6 subtract_subtract_fusion.1
  54.0 0.6 subtract_subtract_fusion
  56.0 0.6 slice-done
  58.9 1.0 %fusion.22 = (f32[6,16,1,130]{3,1,2,0:T(8,128)S(1)}, f32[6,16,1,130]{3,1,0,2:T(8,128)S(1)}, f32[6,16,1,130]{3,1,0,2:T(8,128)S(1)}, f32[6,16,1,130]{3,1,0,2:T(8,1...) fusion(f32[6,16,1,129]{3,1,0,2:T(8,128)S(1)} %slice_bitcast_fus, ...), kind=kLoop, calls=%fused_computation.138 | loop fusion | flops 2882880 | bytes 3045346 | tf_op jit(solution)/shard_map/add | solution.py:123
  60.0 0.8 %fusion.30 = f32[6,16,1,130]{3,1,2,0:T(8,128)S(1)} fusion(f32[6,16,1,129]{3,1,0,2:T(8,128)S(1)} %slice_bitcast_fusion.2, f32[6,16,1,1]{3,1,0,2:T(8,128)S(1)} %slice_bitcast_fusion.16, f32[6,15,1,130]{3,1,0,2:T(8,128)S(1)} %slice_bitcast_fusion.1, f32[6,1,1,130]{3,1,0,2:T(1,128)S(1)} %slice_bitcast_fusion.27, f32[6,16,1,129]{3,1,0,2:T(8,128)S(1)} %fusion.75, ...), kind=kLoop, calls=%fused_computation.146 | loop fusion | flops 2283840 | bytes 2446306 | tf_op jit(solution)/shard_map/add | solution.py:123
  60.8 0.8 %fusion.38 = f32[6,16,1,130]{3,1,2,0:T(8,128)S(1)} fusion(f32[6,16,1,129]{3,1,0,2:T(8,128)S(1)} %slice_bitcast_fusion.5, f32[6,16,1,1]{3,1,0,2:T(8,128)S(1)} %slice_bitcast_fusion.18, f32[6,15,1,130]{3,1,0,2:T(8,128)S(1)} %slice_bitcast_fusion.4, f32[6,1,1,130]{3,1,0,2:T(1,128)S(1)} %slice_bitcast_fusion.28, f32[6,16,1,129]{3,1,0,2:T(8,128)S(1)} %fusion.79, ...), kind=kLoop, calls=%fused_computation.154 | loop fusion | flops 2283840 | bytes 2446306 | tf_op jit(solution)/shard_map/add | solution.py:123
  61.7 0.9 %multiply_add_fusion = (f32[4,16,3,128]{3,1,2,0:T(8,128)}, f32[4,16,3,128]{3,1,2,0:T(8,128)}) fusion(f32[4,16,3,128]{3,1,2,0:T(8,128)S(1)} %copy-done, f32[4,16,3,128]{3,1,2,0:T(8,128)S(1)} %copy-done.4, f32[32,1,128]{2,0,1:T(8,128)S(1)} %bitcast.1032, f32[32,1,128]{2,0,1:T(8,128)S(1)} %bitcast.1033, f32[32,1,128]{2,0,1:T(8,128)S(1)} %bitcast.1031, ...), kind=kOutput, calls=%fused_computation.394 | convolution fusion | flops 9650176 | bytes 592672 | tf_op jit(solution)/shard_map/kp,kcx->pcx/dot_general | solution.py:212
  (182 shorter events, 8.4 us)
Async XLA Ops:
  4.3 8.5 %all-to-all-start = ((f32[8,1,4]{2,1,0:T(1,128)}), f32[8,1,4]{2,1,0:T(1,128)S(1)}, u32[]{:S(2)}, u32[]{:S(2)}) async-start(f32[8,1,4]{2,1,0:T(1,128)} %bitcast.104), calls=%async_computation | async-start | bytes 8192 | tf_op jit(solution)/shard_map/all_to_all | solution.py:198
  9.7 2.7 %copy-start = (f32[4,16,3,128]{3,1,2,0:T(8,128)S(1)}, f32[4,16,3,128]{3,1,2,0:T(8,128)}, u32[]{:S(2)}) copy-start(f32[4,16,3,128]{3,1,2,0:T(8,128)} %param.9) | copy-start | bytes 294916
  10.7 1.7 %copy-start.5 = (f32[1,1,3,16]{3,1,2,0:T(1,128)S(1)}, f32[1,1,3,16]{3,1,2,0:T(1,128)}, u32[]{:S(2)}) copy-start(f32[1,1,3,16]{3,1,2,0:T(1,128)} %param.15) | copy-start | bytes 580
  10.8 8.7 %collective-permute-start = (f32[4,16,5,1]{3,1,0,2:T(8,128)S(1)}, f32[4,16,5,1]{3,1,0,2:T(8,128)S(1)}, u32[]{:S(2)}, u32[]{:S(2)}) collective-permute-start(f32[4,16,5,1]{3,1,0,2:T(8,128)S(1)} %get-tuple-element.109), channel_id=1, source_target_pairs={{0,4},{4,8},{8,12},{12,16},{16,20},{20,24},{24,28},{28,0},{1,5},{5... | collective-permute-start | bytes 3848 | tf_op jit(solution)/shard_map/ppermute | solution.py:42
  10.9 11.0 %collective-permute-start.1 = (f32[4,16,5,1]{3,1,0,2:T(8,128)S(1)}, f32[4,16,5,1]{3,1,0,2:T(8,128)S(1)}, u32[]{:S(2)}, u32[]{:S(2)}) collective-permute-start(f32[4,16,5,1]{3,1,0,2:T(8,128)S(1)} %get-tuple-element.110), channel_id=1, source_target_pairs={{4,0},{8,4},{12,8},{16,12},{20,16},{24,20},{28,24},{0,28},{5,1},{9... | collective-permute-start | bytes 3848 | tf_op jit(solution)/shard_map/ppermute | solution.py:44
  12.7 10.6 %copy-start.1 = (f32[4,16,128]{2,1,0:T(8,128)S(1)}, f32[4,16,128]{2,1,0:T(8,128)}, u32[]{:S(2)}) copy-start(f32[4,16,128]{2,1,0:T(8,128)} %param.12) | copy-start | bytes 98308
  12.7 10.6 %copy-start.2 = (f32[4,16,128]{2,1,0:T(8,128)S(1)}, f32[4,16,128]{2,1,0:T(8,128)}, u32[]{:S(2)}) copy-start(f32[4,16,128]{2,1,0:T(8,128)} %param.11) | copy-start | bytes 98308
  16.6 26.5 %collective-permute-start.10 = (f32[1,4,3,128]{3,1,0,2:T(4,128)S(1)}, f32[1,4,3,128]{3,1,0,2:T(4,128)S(1)}, u32[]{:S(2)}, u32[]{:S(2)}) collective-permute-start(f32[1,4,3,128]{3,1,0,2:T(4,128)S(1)} %get-tuple-element.147), channel_id=1, source_target_pairs={{0,4},{4,8},{8,12},{12,16},{16,20},{20,24},{24,28},{28,0},{1,5},{5... | collective-permute-start | bytes 18440 | tf_op jit(solution)/shard_map/ppermute | solution.py:30
  19.4 23.6 %collective-permute-start.9 = (f32[1,4,3,128]{3,1,0,2:T(4,128)S(1)}, f32[1,4,3,128]{3,1,0,2:T(4,128)S(1)}, u32[]{:S(2)}, u32[]{:S(2)}) collective-permute-start(f32[1,4,3,128]{3,1,0,2:T(4,128)S(1)} %get-tuple-element.148), channel_id=1, source_target_pairs={{0,8},{4,12},{8,16},{12,20},{16,24},{20,28},{24,0},{28,4},{1,9},{5... | collective-permute-start | bytes 18440 | tf_op jit(solution)/shard_map/ppermute | solution.py:30
  19.4 23.6 %collective-permute-start.8 = (f32[1,4,3,128]{3,1,0,2:T(4,128)S(1)}, f32[1,4,3,128]{3,1,0,2:T(4,128)S(1)}, u32[]{:S(2)}, u32[]{:S(2)}) collective-permute-start(f32[1,4,3,128]{3,1,0,2:T(4,128)S(1)} %get-tuple-element.149), channel_id=1, source_target_pairs={{0,12},{4,16},{8,20},{12,24},{16,28},{20,0},{24,4},{28,8},{1,13},{... | collective-permute-start | bytes 18440 | tf_op jit(solution)/shard_map/ppermute | solution.py:30
  19.5 23.6 %collective-permute-start.7 = (f32[1,4,3,128]{3,1,0,2:T(4,128)S(1)}, f32[1,4,3,128]{3,1,0,2:T(4,128)S(1)}, u32[]{:S(2)}, u32[]{:S(2)}) collective-permute-start(f32[1,4,3,128]{3,1,0,2:T(4,128)S(1)} %get-tuple-element.150), channel_id=1, source_target_pairs={{0,16},{4,20},{8,24},{12,28},{16,0},{20,4},{24,8},{28,12},{1,17},{... | collective-permute-start | bytes 18440 | tf_op jit(solution)/shard_map/ppermute | solution.py:30
  21.9 5.2 %collective-permute-start.4 = (f32[1,4,3,128]{3,1,0,2:T(4,128)S(1)}, f32[1,4,3,128]{3,1,0,2:T(4,128)S(1)}, u32[]{:S(2)}, u32[]{:S(2)}) collective-permute-start(f32[1,4,3,128]{3,1,0,2:T(4,128)S(1)} %get-tuple-element.153), channel_id=1, source_target_pairs={{0,28},{4,0},{8,4},{12,8},{16,12},{20,16},{24,20},{28,24},{1,29},{... | collective-permute-start | bytes 18440 | tf_op jit(solution)/shard_map/ppermute | solution.py:30
  27.1 4.3 %collective-permute-start.5 = (f32[1,4,3,128]{3,1,0,2:T(4,128)S(1)}, f32[1,4,3,128]{3,1,0,2:T(4,128)S(1)}, u32[]{:S(2)}, u32[]{:S(2)}) collective-permute-start(f32[1,4,3,128]{3,1,0,2:T(4,128)S(1)} %get-tuple-element.152), channel_id=1, source_target_pairs={{0,24},{4,28},{8,0},{12,4},{16,8},{20,12},{24,16},{28,20},{1,25},{... | collective-permute-start | bytes 18440 | tf_op jit(solution)/shard_map/ppermute | solution.py:30
  31.3 4.3 %collective-permute-start.6 = (f32[1,4,3,128]{3,1,0,2:T(4,128)S(1)}, f32[1,4,3,128]{3,1,0,2:T(4,128)S(1)}, u32[]{:S(2)}, u32[]{:S(2)}) collective-permute-start(f32[1,4,3,128]{3,1,0,2:T(4,128)S(1)} %get-tuple-element.151), channel_id=1, source_target_pairs={{0,20},{4,24},{8,28},{12,0},{16,4},{20,8},{24,12},{28,16},{1,21},{... | collective-permute-start | bytes 18440 | tf_op jit(solution)/shard_map/ppermute | solution.py:30
  35.6 11.6 %collective-permute-start.2 = (f32[1,16,5,130]{3,1,0,2:T(8,128)S(1)}, f32[1,16,5,130]{3,1,0,2:T(8,128)S(1)}, u32[]{:S(2)}, u32[]{:S(2)}) collective-permute-start(f32[1,16,5,130]{3,1,0,2:T(8,128)S(1)} %get-tuple-element.107), channel_id=1, source_target_pairs={{0,1},{1,2},{2,3},{3,0},{4,5},{5,6},{6,7},{7,4},{8,9},{9,10},{10,1... | collective-permute-start | bytes 124808 | tf_op jit(solution)/shard_map/ppermute | solution.py:42
  43.0 4.2 %collective-permute-start.3 = (f32[1,16,5,130]{3,1,0,2:T(8,128)S(1)}, f32[1,16,5,130]{3,1,0,2:T(8,128)S(1)}, u32[]{:S(2)}, u32[]{:S(2)}) collective-permute-start(f32[1,16,5,130]{3,1,0,2:T(8,128)S(1)} %get-tuple-element.108), channel_id=1, source_target_pairs={{1,0},{2,1},{3,2},{0,3},{5,4},{6,5},{7,6},{4,7},{9,8},{10,9},{11,1... | collective-permute-start | bytes 124808 | tf_op jit(solution)/shard_map/ppermute | solution.py:44
  54.6 1.3 %copy-start.3 = (f32[6,16,130]{2,1,0:T(8,128)}, f32[6,16,130]{2,1,0:T(8,128)S(1)}, u32[]{:S(2)}) copy-start(f32[6,16,130]{2,1,0:T(8,128)S(1)} %subtract_subtract_fusion) | copy-start | bytes 149764
  55.9 0.7 %slice-start = ((f32[6,16,130]{2,1,0:T(8,128)}), f32[1,16,130]{2,1,0:T(8,128)S(1)}, s32[]{:S(2)}) async-start(f32[6,16,130]{2,1,0:T(8,128)} %copy-done.3), calls=%async_computation.1 | async-start | bytes 32768 | tf_op jit(solution)/shard_map/jit(_roll_static)/slice | solution.py:123
  55.9 0.9 %slice-start.1 = ((f32[6,16,130]{2,1,0:T(8,128)}), f32[5,16,130]{2,1,0:T(8,128)S(1)}, s32[]{:S(2)}) async-start(f32[6,16,130]{2,1,0:T(8,128)} %copy-done.3), calls=%async_computation.2 | async-start | bytes 163840 | tf_op jit(solution)/shard_map/jit(_roll_static)/slice | solution.py:123
  60.8 0.9 %copy-start.4 = (f32[4,16,3,128]{3,1,2,0:T(8,128)S(1)}, f32[4,16,3,128]{3,1,2,0:T(8,128)}, u32[]{:S(2)}) copy-start(f32[4,16,3,128]{3,1,2,0:T(8,128)} %param.10) | copy-start | bytes 294916
